TPU v7x, 32 devices: a whole 2x2x4 slice. The times are simulated.
32 devices in a mesh: req: 8 (over y, x, core), mdl: 4 (over z).
Axes of the slice: x: 2, y: 2, z: 4, core: 2. Of those that a mesh axis runs over, the one named last changes fastest.
Arguments:
- tokens: bfloat16 [256, 4, 2048], P('req', None, 'mdl'), may hold values from -6 to 6
- counts: int32 [256], P('req'), may hold values from 1 to 4
- new_owner: int32 [256], replicated, may hold values from 0 to 255, as said below
- wkv_state: float32 [256, 32, 4096], P('req', 'mdl'), may hold values from -12 to 12
- att_shift: bfloat16 [256, 2048], P('req', 'mdl'), may hold values from -6 to 6
- ffn_shift: bfloat16 [256, 2048], P('req', 'mdl'), may hold values from -6 to 6
- norm_params: float32 [4, 2048], replicated, may hold values from 0.25 to 1.75
- mix_coeffs: float32 [7, 2048], replicated, may hold values from 0 to 1
- head_params: float32 [7, 2048], P(None, 'mdl'), may hold values from -6 to 2
- recept_weight: bfloat16 [2048, 2048], P(None, 'mdl'), may hold values from -0.125 to 0.125
- key_weight: bfloat16 [2048, 2048], P(None, 'mdl'), may hold values from -0.125 to 0.125
- value_weight: bfloat16 [2048, 2048], P(None, 'mdl'), may hold values from -0.125 to 0.125
- output_weight: bfloat16 [2048, 2048], P('mdl'), may hold values from -0.125 to 0.125
- decay_down: bfloat16 [2048, 96], P('mdl'), may hold values from -0.125 to 0.125
- decay_up: bfloat16 [96, 2048], P(None, 'mdl'), may hold values from -0.625 to 0.625
- alpha_down: bfloat16 [2048, 96], P('mdl'), may hold values from -0.125 to 0.125
- alpha_up: bfloat16 [96, 2048], P(None, 'mdl'), may hold values from -0.625 to 0.625
- gate_down: bfloat16 [2048, 256], P('mdl'), may hold values from -0.125 to 0.125
- gate_up: bfloat16 [256, 2048], P(None, 'mdl'), may hold values from -0.375 to 0.375
- ffn_key_weight: bfloat16 [2048, 4096], P(None, 'mdl'), may hold values from -0.125 to 0.125
- ffn_value_weight: bfloat16 [4096, 2048], P('mdl'), may hold values from -0.09375 to 0.09375
Outputs:
- block_output: bfloat16 [256, 4, 2048], P('req', None, 'mdl')
- new_state: float32 [256, 32, 4096], P('req', 'mdl')
- new_att_shift: bfloat16 [256, 2048], P('req', 'mdl')
- new_ffn_shift: bfloat16 [256, 2048], P('req', 'mdl')
Inputs may be any that keep to these rules, and one draw needn't show every extreme that they name: new_owner is a permutation: the states of request i move to position new_owner[i]. Of the 32 requests of each aligned block of positions, exactly 4 move into each aligned block.
All inputs are finite; a program needn't handle non-finite values.
Results may differ from a plain program's by a relative error of at most 0.0095.
Values may be sent and summed in bfloat16 or wider, within the bound.
No kernel may reach another device: no remote copies, remote signals or barrier semaphores. Data moves between devices by JAX's collectives and lax.ppermute only.
A program may use at most 256 MiB of HBM per device.

v0:
```python
import jax
import jax.numpy as jnp
from jax import lax
from jax.sharding import PartitionSpec as P


def layer_norm(stream, gain_row, offset):
    center = stream - jnp.mean(stream, axis=-1, keepdims=True)
    spread = jnp.mean(center * center, axis=-1, keepdims=True)
    return center / jnp.sqrt(spread + 1e-05) * gain_row + offset


def project(inputs, weight):
    return jnp.dot(inputs, weight, preferred_element_type=jnp.float32)


def split_heads(source, head_size):
    sequence_batch_count, decode_loop_steps_count, feature_count = source.shape
    return source.reshape(
        sequence_batch_count, decode_loop_steps_count, feature_count // head_size, head_size
    )


def advance(wkv_square, decay_now, key_now, value_now, unit_now, alpha_now, recept_now, is_valid):
    removal = -jnp.sum(wkv_square * unit_now[:, :, None, :], axis=-1)
    updated = (
        wkv_square * decay_now[:, :, None, :]
        + removal[..., None] * (unit_now * alpha_now)[:, :, None, :]
        + value_now[..., None] * key_now[:, :, None, :]
    )
    memory_matrix_product = jnp.sum(updated * recept_now[:, :, None, :], axis=-1)
    return (jnp.where(is_valid[:, None, None, None], updated, wkv_square), memory_matrix_product)


def prepare_keys(key_proj, in_context, learned_weights, head_size):
    scaled = split_heads(key_proj * learned_weights[2], head_size)
    key_unit = scaled / jnp.sqrt(jnp.sum(scaled * scaled, axis=-1, keepdims=True) + 1e-06)
    lookup_adjust_factor = key_proj * (1.0 + (in_context - 1.0) * learned_weights[3])
    return (key_unit.reshape(key_proj.shape), lookup_adjust_factor)


def run_heads(
    wkv_flat,
    decay_rate,
    lookup_adjust_factor,
    values,
    key_unit,
    in_context,
    acceptance_matrix_lines,
    live_mask,
    head_size,
):
    sequence_batch_count, decode_loop_steps_count, feature_count = acceptance_matrix_lines.shape
    head_count = feature_count // head_size
    decay_heads = split_heads(decay_rate, head_size)
    keymod_heads = split_heads(lookup_adjust_factor, head_size)
    payload_each_group = split_heads(values, head_size)
    unit_heads = split_heads(key_unit, head_size)
    alpha_heads = split_heads(in_context, head_size)
    recept_heads = split_heads(acceptance_matrix_lines, head_size)
    wkv_square = wkv_flat.reshape(sequence_batch_count, head_count, head_size, head_size)
    readouts = []
    for position in range(decode_loop_steps_count):
        wkv_square, memory_matrix_product = advance(
            wkv_square,
            decay_heads[:, position],
            keymod_heads[:, position],
            payload_each_group[:, position],
            unit_heads[:, position],
            alpha_heads[:, position],
            recept_heads[:, position],
            live_mask[:, position] > 0.5,
        )
        readouts.append(memory_matrix_product)
    stacked = jnp.stack(readouts, axis=1).reshape(
        sequence_batch_count, decode_loop_steps_count, feature_count
    )
    return (stacked, wkv_square.reshape(sequence_batch_count, head_count, head_size * head_size))


def finish_heads(
    memory_matrix_product,
    acceptance_matrix_lines,
    lookup_adjust_factor,
    values,
    sigmoid_scaling_entries,
    learned_weights,
    head_size,
):
    stacked = split_heads(memory_matrix_product, head_size)
    center = stacked - jnp.mean(stacked, axis=-1, keepdims=True)
    spread = jnp.mean(center * center, axis=-1, keepdims=True)
    layernormed_activations = (center / jnp.sqrt(spread + 0.00064)).reshape(
        memory_matrix_product.shape
    ) * learned_weights[5] + learned_weights[6]
    extra_term_share = jnp.sum(
        split_heads(acceptance_matrix_lines * lookup_adjust_factor * learned_weights[4], head_size),
        axis=-1,
        keepdims=True,
    ) * split_heads(values, head_size)
    return (
        (layernormed_activations + extra_term_share.reshape(memory_matrix_product.shape))
        * sigmoid_scaling_entries
    ).astype(jnp.bfloat16)


def per_device(
    tokens,
    counts,
    new_owner,
    wkv_state,
    att_shift,
    ffn_shift,
    norm_params,
    mix_coeffs,
    head_params,
    recept_weight,
    key_weight,
    value_weight,
    output_weight,
    decay_down,
    decay_up,
    alpha_down,
    alpha_up,
    gate_down,
    gate_up,
    ffn_key_weight,
    ffn_value_weight,
):
    groups = lax.axis_size("req")
    sequence_batch_count, decode_loop_steps_count, local_width = tokens.shape
    per_pair = sequence_batch_count // groups
    req_rank = lax.axis_index("req")
    column_start = lax.axis_index("mdl") * local_width
    head_size = local_width // wkv_state.shape[1]
    row_count = sequence_batch_count * decode_loop_steps_count
    shape_three = (sequence_batch_count, decode_loop_steps_count, local_width)
    slot_ids = jnp.arange(decode_loop_steps_count, dtype=jnp.int32)
    live_mask = (slot_ids[None, :] < counts[:, None]).astype(jnp.float32)
    own_block = lax.dynamic_slice_in_dim(
        new_owner, req_rank * sequence_batch_count, sequence_batch_count
    )
    sending = jnp.argsort(own_block)
    sorted_rows = jnp.sort(new_owner.reshape(groups, sequence_batch_count), axis=1)
    arriving = (
        lax.dynamic_slice_in_dim(sorted_rows, req_rank * per_pair, per_pair, 1)
        - req_rank * sequence_batch_count
    )
    placing = jnp.argsort(arriving.reshape(-1))
    sent_state = wkv_state[sending].reshape((groups, per_pair) + wkv_state.shape[1:])
    sent_att = att_shift[sending].astype(jnp.float32).reshape(groups, per_pair, local_width)
    sent_ffn = ffn_shift[sending].astype(jnp.float32).reshape(groups, per_pair, local_width)
    got_state, got_att, got_ffn = (
        lax.all_to_all(sent_state, "req", split_axis=0, concat_axis=0, tiled=True),
        lax.all_to_all(sent_att, "req", split_axis=0, concat_axis=0, tiled=True),
        lax.all_to_all(sent_ffn, "req", split_axis=0, concat_axis=0, tiled=True),
    )
    moved_state = got_state.reshape((sequence_batch_count,) + wkv_state.shape[1:])[placing]
    moved_att = got_att.reshape(sequence_batch_count, local_width)[placing].astype(jnp.bfloat16)
    moved_ffn = got_ffn.reshape(sequence_batch_count, local_width)[placing].astype(jnp.bfloat16)
    full_tokens = lax.all_gather(tokens, "mdl", axis=2, tiled=True)
    full_stream = full_tokens.astype(jnp.float32)
    entire_channel_count = full_tokens.shape[2]
    prev_att, prev_ffn = (
        lax.all_gather(moved_att, "mdl", axis=1, tiled=True),
        lax.all_gather(moved_ffn, "mdl", axis=1, tiled=True),
    )
    normed_one = layer_norm(full_stream, norm_params[0], norm_params[1])
    before_one = jnp.concatenate(
        [prev_att.astype(jnp.float32)[:, None], normed_one[:, :-1]], axis=1
    )
    delta_one = before_one - normed_one
    normed_local = lax.dynamic_slice_in_dim(normed_one, column_start, local_width, 2)

    def mixed_input(mix_index):
        return (
            (normed_one + delta_one * mix_coeffs[mix_index])
            .astype(jnp.bfloat16)
            .reshape(row_count, entire_channel_count)
        )

    decay_full, alpha_full, gate_full = (
        lax.all_gather(decay_down, "mdl", axis=0, tiled=True),
        lax.all_gather(alpha_down, "mdl", axis=0, tiled=True),
        lax.all_gather(gate_down, "mdl", axis=0, tiled=True),
    )
    decay_sum = project(mixed_input(1), decay_full)
    alpha_sum = project(mixed_input(4), alpha_full)
    gate_sum = project(mixed_input(5), gate_full)
    decay_low = jnp.tanh(decay_sum).astype(jnp.bfloat16)
    alpha_low = alpha_sum.astype(jnp.bfloat16)
    gate_low = jax.nn.sigmoid(gate_sum).astype(jnp.bfloat16)
    decay_rate = jnp.exp(
        -0.606531 * jax.nn.sigmoid(head_params[0] + project(decay_low, decay_up))
    ).reshape(shape_three)
    in_context = jax.nn.sigmoid(head_params[1] + project(alpha_low, alpha_up)).reshape(shape_three)
    sigmoid_scaling_entries = project(gate_low, gate_up).reshape(shape_three)
    acceptance_matrix_lines = project(mixed_input(0), recept_weight).reshape(shape_three)
    key_proj = project(mixed_input(2), key_weight).reshape(shape_three)
    values = project(mixed_input(3), value_weight).reshape(shape_three)
    key_unit, lookup_adjust_factor = prepare_keys(key_proj, in_context, head_params, head_size)
    memory_matrix_product, new_state = run_heads(
        moved_state,
        decay_rate,
        lookup_adjust_factor,
        values,
        key_unit,
        in_context,
        acceptance_matrix_lines,
        live_mask,
        head_size,
    )
    attention_group_result = finish_heads(
        memory_matrix_product,
        acceptance_matrix_lines,
        lookup_adjust_factor,
        values,
        sigmoid_scaling_entries,
        head_params,
        head_size,
    )
    attended_term = project(attention_group_result.reshape(row_count, local_width), output_weight)
    attended = lax.psum_scatter(attended_term, "mdl", scatter_dimension=1, tiled=True).reshape(
        shape_three
    )
    midstream = (tokens.astype(jnp.float32) + attended).astype(jnp.bfloat16)
    full_mid = lax.all_gather(midstream, "mdl", axis=2, tiled=True)
    normed_two = layer_norm(full_mid.astype(jnp.float32), norm_params[2], norm_params[3])
    before_two = jnp.concatenate(
        [prev_ffn.astype(jnp.float32)[:, None], normed_two[:, :-1]], axis=1
    )
    ffn_in = (
        (normed_two + (before_two - normed_two) * mix_coeffs[6])
        .astype(jnp.bfloat16)
        .reshape(row_count, entire_channel_count)
    )
    hidden = jnp.square(jax.nn.relu(project(ffn_in, ffn_key_weight))).astype(jnp.bfloat16)
    ffn_out = (
        lax.psum_scatter(
            project(hidden, ffn_value_weight).astype(jnp.bfloat16),
            "mdl",
            scatter_dimension=1,
            tiled=True,
        )
        .astype(jnp.float32)
        .reshape(shape_three)
    )
    block_output = jnp.where(
        live_mask[..., None] > 0.5, midstream.astype(jnp.float32) + ffn_out, 0.0
    ).astype(jnp.bfloat16)
    chosen = (slot_ids[None, :] == (counts - 1)[:, None]).astype(jnp.float32)
    normed_two_local = lax.dynamic_slice_in_dim(normed_two, column_start, local_width, 2)
    new_att_shift = jnp.sum(normed_local * chosen[..., None], axis=1).astype(jnp.bfloat16)
    new_ffn_shift = jnp.sum(normed_two_local * chosen[..., None], axis=1).astype(jnp.bfloat16)
    return (block_output, new_state, new_att_shift, new_ffn_shift)


def solution(mesh):
    return jax.shard_map(
        per_device,
        mesh=mesh,
        in_specs=(
            P("req", None, "mdl"),
            P("req"),
            P(),
            P("req", "mdl", None),
            P("req", "mdl"),
            P("req", "mdl"),
            P(),
            P(),
            P(None, "mdl"),
            P(None, "mdl"),
            P(None, "mdl"),
            P(None, "mdl"),
            P("mdl", None),
            P("mdl", None),
            P(None, "mdl"),
            P("mdl", None),
            P(None, "mdl"),
            P("mdl", None),
            P(None, "mdl"),
            P(None, "mdl"),
            P("mdl", None),
        ),
        out_specs=(P("req", None, "mdl"), P("req", "mdl", None), P("req", "mdl"), P("req", "mdl")),
        check_vma=False,
    )
```

profile of v0, /device:TPU:0, one launch (start us, length us, event | category | flops | bytes accessed | tf_op | source)
XLA Modules:
  0.0 439.1 jit_solution(6680961267923316029)
XLA Ops:
  12.3 5.2 %all-to-all-start.1 = ((bf16[8,4,512]{2,1,0:T(4,128)(2,1)}), bf16[8,4,512]{2,1,0:T(4,128)(2,1)S(1)}, u32[]{:S(2)}, u32[]{:S(2)}) async-start(bf16[8,4,512]{2,1,0:T(4,128)(2,1)} %reshape.354), calls=%async_computation.1 | async-start | bytes 65536 | tf_op jit(solution)/shard_map/all_to_all | solution.py:155
  27.7 20.2 %all_gather.23 = bf16[2048,96]{0,1:T(8,128)(2,1)} all-gather(bf16[512,96]{0,1:T(8,128)(2,1)} %param.34), channel_id=1, replica_groups=mesh['req'=8,'mdl'=4] {'mdl'}, dimensions={0}, use_global_device_ids=true | all-gather | bytes 491520 | tf_op jit(solution)/shard_map/all_gather | solution.py:183
  47.9 15.2 %all_gather.24 = bf16[2048,96]{0,1:T(8,128)(2,1)S(1)} all-gather(bf16[512,96]{0,1:T(8,128)(2,1)} %param.36), channel_id=1, replica_groups=mesh['req'=8,'mdl'=4] {'mdl'}, dimensions={0}, use_global_device_ids=true | all-gather | bytes 491520 | tf_op jit(solution)/shard_map/all_gather | solution.py:184
  63.2 14.9 %all_gather.21 = bf16[32,4,2048]{2,1,0:T(4,128)(2,1)S(1)} all-gather(bf16[32,4,512]{2,1,0:T(4,128)(2,1)} %param.21), channel_id=1, replica_groups=mesh['req'=8,'mdl'=4] {'mdl'}, dimensions={2}, use_global_device_ids=true | all-gather | bytes 655360 | tf_op jit(solution)/shard_map/all_gather | solution.py:161
  80.4 3.9 copy.89
  84.3 5.0 %gather_fusion = f32[32,8,4096]{2,1,0:T(8,128)} fusion(f32[32,8,4096]{2,1,0:T(8,128)} %param.24, s32[1024]{0:T(1024)S(1)} %pad_clamp_fusion.1), kind=kCustom, calls=%fused_computation | custom fusion | bytes 8388736 | tf_op jit(solution)/shard_map/gather | solution.py:150
  89.4 4.8 %all-to-all-start = ((f32[8,4,8,4096]{3,2,1,0:T(8,128)}), f32[8,4,8,4096]{3,2,1,0:T(8,128)}, u32[]{:S(2)}, u32[]{:S(2)}) async-start(f32[8,4,8,4096]{3,2,1,0:T(8,128)} %bitcast.175), calls=%async_computation | async-start | bytes 8388608 | tf_op jit(solution)/shard_map/all_to_all | solution.py:154
  94.9 13.7 %all_gather.22 = bf16[32,2048]{1,0:T(8,128)(2,1)S(1)} all-gather(bf16[32,512]{1,0:T(8,128)(2,1)S(1)} %gather_fusion.3), channel_id=1, replica_groups=mesh['req'=8,'mdl'=4] {'mdl'}, dimensions={1}, use_global_device_ids=true | all-gather | bytes 163840 | tf_op jit(solution)/shard_map/all_gather | solution.py:165
  108.8 3.5 add_convert_fusion.1
  112.3 2.0 reshape.344
  114.3 2.2 fusion.61
  118.2 1.9 reshape.348
  120.2 4.4 %add_convert_fusion.5 = (bf16[32,4,2048]{2,1,0:T(4,128)(2,1)}, bf16[32,4,2048]{2,1,0:T(4,128)(2,1)}, bf16[32,4,2048]{2,1,0:T(4,128)(2,1)}, bf16[32,4,2048,1]{2,1,0,3:T(4,128)(2,1)}) fusion(f32[2048]{0:T(1024)} %bitcast.202, f32[32,3,2048]{2,1,0:T(4,128)} %bitcast.177, f32[32,1,2048]{2,1,0:T(1,128)S(1)} %copy.86, f32[2048]{0:T(1024)} %bitcast.190, ...), kind=kLoop, calls=%fused_computation.82 | loop fusion | flops 4980736 | bytes 3720192 | tf_op jit(solution)/shard_map/convert_element_type | solution.py:178
  129.6 2.2 broadcast_add_fusion
  131.8 2.5 fusion.39
  137.0 3.8 broadcast_multiply_fusion.8
  154.7 2.3 fusion.23
  157.1 5.1 %gather_fusion.1 = f32[32,8,4096]{2,1,0:T(8,128)} fusion(f32[32,8,4096]{2,1,0:T(8,128)} %bitcast.1, s32[1024]{0:T(1024)} %copy-done.21), kind=kCustom, calls=%fused_computation.1 | custom fusion | bytes 8388736 | tf_op jit(solution)/shard_map/gather | solution.py:158
  162.2 8.3 %reshape.338 = f32[32,8,64,64]{3,2,1,0:T(8,128)} reshape(f32[32,8,4096]{2,1,0:T(8,128)} %gather_fusion.1) | data formatting | bytes 8388608 | tf_op jit(solution)/shard_map/reshape | solution.py:61
  170.5 5.8 %multiply_reduce_fusion.7 = f32[32,8,64]{2,1,0:T(8,128)S(1)} fusion(f32[32,8,64,64]{3,2,1,0:T(8,128)} %reshape.338, f32[32,8,64]{2,1,0:T(8,128)S(1)} %get-tuple-element.90), kind=kLoop, calls=%fused_computation.16 | loop fusion | flops 2080768 | bytes 4325376 | tf_op jit(solution)/shard_map/reduce_sum | solution.py:25
  176.4 11.0 %multiply_reduce_fusion.6 = (f32[32,8,64]{2,1,0:T(8,128)S(1)}, f32[32,8,64]{2,1,0:T(8,128)S(1)}) fusion(f32[32,8,64]{2,1,0:T(8,128)S(1)} %copy-done.8, f32[32,8,64,64]{3,2,1,0:T(8,128)S(1)} %copy-done.2, f32[32,8,64]{2,1,0:T(8,128)S(1)} %get-tuple-element.51, f32[32,8,64]{2,1,0:T(8,128)S(1)} %get-tuple-element.30, f32[32,8,64]{2,1,0:T(8,128)S(1)} %neg.38, ...), kind=kLoop, calls=%fused_computation.14 | loop fusion | flops 10452992 | bytes 4784160 | tf_op jit(solution)/shard_map/reduce_sum | solution.py:31
  188.8 18.7 %multiply_reduce_fusion.3 = (f32[32,8,64]{2,1,0:T(8,128)S(1)}, f32[32,8,64,64]{3,2,1,0:T(8,128)}, f32[32,8,64]{2,1,0:T(8,128)S(1)}, f32[32,8,64,64]{3,2,1,0:T(8,...) fusion(f32[32,8,64]{2,1,0:T(8,128)} %get-tuple-element.92, ...), kind=kLoop, calls=%fused_computation.10 | loop fusion | flops 16744448 | bytes 26083392 | tf_op jit(solution)/shard_map/reduce_sum | solution.py:25
  208.3 12.5 %multiply_reduce_fusion.2 = (f32[32,8,64]{2,1,0:T(8,128)S(1)}, f32[32,8,64]{2,1,0:T(8,128)S(1)}, f32[32,8,64,64]{3,2,1,0:T(8,128)}, f32[32,8,64,64]{3,2,1,0:T(8,128)}) fusion(f32[32,8,64]{2,1,0:T(8,128)} %get-tuple-element.34, f32[32,8,64,64]{3,2,1,0:T(8,128)} %get-tuple-element.18, f32[32,8,64]{2,1,0:T(8,128)S(1)} %get-tuple-element.48, ...), kind=kLoop, calls=%fused_computation.8 | loop fusion | flops 10452992 | bytes 13172768 | tf_op jit(solution)/shard_map/reduce_sum | solution.py:31
  222.2 15.5 %broadcast_multiply_fusion.1 = (f32[32,8,64,64]{3,2,1,0:T(8,128)}, f32[32,8,64]{2,1,0:T(8,128)S(1)}, f32[32,8,64,64]{3,2,1,0:T(8,128)}) fusion(f32[32,8,64]{2,1,0:T(8,128)} %get-tuple-element.31, f32[32,8,64]{2,1,0:T(8,128)} %neg.42, f32[32,8,64]{2,1,0:T(8,128)} %get-tuple-element.33, f32[32,8,64]{2,1,0:T(8,128)} %get-tuple-element.40, ...), kind=kLoop, calls=%fused_computation.19 | loop fusion | flops 13615104 | bytes 13369376 | tf_op jit(solution)/shard_map/mul | solution.py:28
  242.0 2.8 fusion.19
  246.2 4.5 %all-to-all-start.2 = ((bf16[8,4,512]{2,1,0:T(4,128)(2,1)}), bf16[8,4,512]{2,1,0:T(4,128)(2,1)S(1)}, u32[]{:S(2)}, u32[]{:S(2)}) async-start(bf16[8,4,512]{2,1,0:T(4,128)(2,1)} %reshape.356), calls=%async_computation.3 | async-start | bytes 65536 | tf_op jit(solution)/shard_map/all_to_all | solution.py:156
  250.9 4.6 %all-to-all-done.2 = bf16[8,4,512]{2,1,0:T(4,128)(2,1)S(1)} async-done(((bf16[8,4,512]{2,1,0:T(4,128)(2,1)}), bf16[8,4,512]{2,1,0:T(4,128)(2,1)S(1)}, u32[]{:S(2)}, u32[]{:S(2)}) %all-to-all-start.2) | async-done | bytes 32800 | tf_op jit(solution)/shard_map/all_to_all | solution.py:156
  256.3 14.6 %all_gather.27 = bf16[32,2048]{1,0:T(8,128)(2,1)S(1)} all-gather(bf16[32,512]{1,0:T(8,128)(2,1)S(1)} %gather_fusion.5), channel_id=1, replica_groups=mesh['req'=8,'mdl'=4] {'mdl'}, dimensions={1}, use_global_device_ids=true | all-gather | bytes 163840 | tf_op jit(solution)/shard_map/all_gather | solution.py:166
  271.2 3.7 mul.597
  274.9 8.1 %mul.647 = f32[32,8,4096]{2,1,0:T(8,128)} reshape(f32[32,8,64,64]{3,2,1,0:T(8,128)} %mul.597) | data formatting | bytes 8388608 | tf_op jit(solution)/shard_map/mul | solution.py:27
  283.0 3.7 mul.561
  286.7 7.9 %mul.639 = f32[32,8,4096]{2,1,0:T(8,128)} reshape(f32[32,8,64,64]{3,2,1,0:T(8,128)} %mul.561) | data formatting | bytes 8388608 | tf_op jit(solution)/shard_map/mul | solution.py:27
  294.6 3.7 mul.579
  298.3 7.9 %mul.643 = f32[32,8,4096]{2,1,0:T(8,128)} reshape(f32[32,8,64,64]{3,2,1,0:T(8,128)} %mul.579) | data formatting | bytes 8388608 | tf_op jit(solution)/shard_map/mul | solution.py:27
  306.2 3.7 mul.523
  309.9 7.9 %mul.635 = f32[32,8,4096]{2,1,0:T(8,128)} reshape(f32[32,8,64,64]{3,2,1,0:T(8,128)} %mul.523) | data formatting | bytes 8388608 | tf_op jit(solution)/shard_map/mul | solution.py:27
  317.8 7.9 %mul.637 = f32[32,8,4096]{2,1,0:T(8,128)} reshape(f32[32,8,64,64]{3,2,1,0:T(8,128)} %get-tuple-element.52) | data formatting | bytes 8388608 | tf_op jit(solution)/shard_map/mul | solution.py:28
  325.7 7.9 %mul.638 = f32[32,8,4096]{2,1,0:T(8,128)} reshape(f32[32,8,64,64]{3,2,1,0:T(8,128)} %get-tuple-element.53) | data formatting | bytes 8388608 | tf_op jit(solution)/shard_map/mul | solution.py:29
  333.6 7.9 %mul.641 = f32[32,8,4096]{2,1,0:T(8,128)} reshape(f32[32,8,64,64]{3,2,1,0:T(8,128)} %get-tuple-element.54) | data formatting | bytes 8388608 | tf_op jit(solution)/shard_map/mul | solution.py:28
  341.5 7.9 %mul.642 = f32[32,8,4096]{2,1,0:T(8,128)} reshape(f32[32,8,64,64]{3,2,1,0:T(8,128)} %get-tuple-element.55) | data formatting | bytes 8388608 | tf_op jit(solution)/shard_map/mul | solution.py:29
  349.4 7.9 %mul.645 = f32[32,8,4096]{2,1,0:T(8,128)} reshape(f32[32,8,64,64]{3,2,1,0:T(8,128)} %get-tuple-element.56) | data formatting | bytes 8388608 | tf_op jit(solution)/shard_map/mul | solution.py:28
  357.3 7.9 %mul.646 = f32[32,8,4096]{2,1,0:T(8,128)} reshape(f32[32,8,64,64]{3,2,1,0:T(8,128)} %get-tuple-element.57) | data formatting | bytes 8388608 | tf_op jit(solution)/shard_map/mul | solution.py:29
  365.2 7.9 %mul.649 = f32[32,8,4096]{2,1,0:T(8,128)} reshape(f32[32,8,64,64]{3,2,1,0:T(8,128)} %get-tuple-element.58) | data formatting | bytes 8388608 | tf_op jit(solution)/shard_map/mul | solution.py:28
  373.1 7.9 %mul.650 = f32[32,8,4096]{2,1,0:T(8,128)} reshape(f32[32,8,64,64]{3,2,1,0:T(8,128)} %get-tuple-element.60) | data formatting | bytes 8388608 | tf_op jit(solution)/shard_map/mul | solution.py:29
  382.2 16.0 %all_gather.26 = bf16[32,4,2048]{2,1,0:T(4,128)(2,1)S(1)} all-gather(bf16[32,4,512]{2,1,0:T(4,128)(2,1)S(1)} %add_convert_fusion.6), channel_id=1, replica_groups=mesh['req'=8,'mdl'=4] {'mdl'}, dimensions={2}, use_global_device_ids=true | all-gather | bytes 655360 | tf_op jit(solution)/shard_map/all_gather | solution.py:227
  400.7 5.6 %convolution_convert_fusion = bf16[128,2048]{1,0:T(8,128)(2,1)} fusion(bf16[1024,2048]{1,0:T(8,128)(2,1)} %param.41, bf16[128,2048]{1,0:T(8,128)(2,1)S(1)} %reshape.351, bf16[2048,1024]{1,0:T(8,128)(2,1)} %param.40), kind=kOutput, calls=%fused_computation.29 | convolution fusion | flops 1074397184 | bytes 9437184 | tf_op jit(solution)/shard_map/dot_general | solution.py:14
  406.3 22.3 %add_select_fusion = f32[32,8,4096]{2,1,0:T(8,128)} fusion(f32[32,8,4096]{2,1,0:T(8,128)} %mul.650, f32[32,8,4096]{2,1,0:T(8,128)} %mul.649, f32[32,8,4096]{2,1,0:T(8,128)} %mul.647, f32[32,8,4096]{2,1,0:T(8,128)} %mul.646, f32[32,8,4096]{2,1,0:T(8,128)} %mul.645, f32[32,8,4096]{2,1,0:T(8,128)} %mul.643, f32[32,8,4096]{2,1,0:T(8,128)} %mul.642, ...), kind=kLoop, calls=%fused_computation.17 | loop fusion | flops 16777216 | bytes 58720384 | tf_op jit(solution)/shard_map/jit(_where)/select_n | solution.py:32
  428.6 2.0 multiply_reduce_fusion.10
  (162 shorter events, 57.8 us)
Async XLA Ops:
  7.2 234.8 %copy-start = (bf16[512,2048]{1,0:T(8,128)(2,1)S(1)}, bf16[512,2048]{1,0:T(8,128)(2,1)}, u32[]{:S(2)}) copy-start(bf16[512,2048]{1,0:T(8,128)(2,1)} %param.33) | copy-start | bytes 6291460
  7.2 147.5 %all-gather.2.cloned.1.call-start = ((), (), s32[]{:S(2)}) async-start(), calls=%async_computation.5 | async-start | bytes 1310720 | tf_op jit(solution)/shard_map/all_gather | solution.py:185
  10.3 79.1 %copy-start.20 = (s32[1024]{0:T(1024)}, s32[1024]{0:T(1024)S(1)}, u32[]{:S(2)}) copy-start(s32[1024]{0:T(1024)S(1)} %pad_clamp_fusion.1) | copy-start | bytes 12292
  12.3 77.0 %all-to-all-start.1 = ((bf16[8,4,512]{2,1,0:T(4,128)(2,1)}), bf16[8,4,512]{2,1,0:T(4,128)(2,1)S(1)}, u32[]{:S(2)}, u32[]{:S(2)}) async-start(bf16[8,4,512]{2,1,0:T(4,128)(2,1)} %reshape.354), calls=%async_computation.1 | async-start | bytes 65536 | tf_op jit(solution)/shard_map/all_to_all | solution.py:155
  25.9 63.5 %copy-start.11 = (f32[1,2048]{1,0:T(1,128)}, f32[1,2048]{1,0:T(1,128)S(1)}, u32[]{:S(2)}) copy-start(f32[1,2048]{1,0:T(1,128)S(1)} %get-tuple-element.70) | copy-start | bytes 24580
  25.9 63.5 %copy-start.12 = (f32[1,2048]{1,0:T(1,128)}, f32[1,2048]{1,0:T(1,128)S(1)}, u32[]{:S(2)}) copy-start(f32[1,2048]{1,0:T(1,128)S(1)} %get-tuple-element.71) | copy-start | bytes 24580
  78.9 10.5 %copy-start.10 = (f32[32,4]{1,0:T(8,128)}, f32[32,4]{1,0:T(8,128)S(1)}, u32[]{:S(2)}) copy-start(f32[32,4]{1,0:T(8,128)S(1)} %add_sqrt_fusion.3) | copy-start | bytes 1540
  80.4 13.8 %copy-start.21 = (s32[1024]{0:T(1024)}, s32[1024]{0:T(1024)S(1)}, u32[]{:S(2)}) copy-start(s32[1024]{0:T(1024)S(1)} %pad_clamp_fusion) | copy-start | bytes 12292
  89.4 67.7 %all-to-all-start = ((f32[8,4,8,4096]{3,2,1,0:T(8,128)}), f32[8,4,8,4096]{3,2,1,0:T(8,128)}, u32[]{:S(2)}, u32[]{:S(2)}) async-start(f32[8,4,8,4096]{3,2,1,0:T(8,128)} %bitcast.175), calls=%async_computation | async-start | bytes 8388608 | tf_op jit(solution)/shard_map/all_to_all | solution.py:154
  94.2 286.9 %reduce-scatter.3.cloned.1.call-start = ((), (), s32[]{:S(2)}) async-start(), calls=%async_computation.6 | async-start | bytes 1310720 | tf_op jit(solution)/shard_map/reduce_scatter | solution.py:223
  162.2 14.1 %copy-start.5 = (f32[32,8,64]{2,1,0:T(8,128)S(1)}, f32[32,8,64]{2,1,0:T(8,128)}, u32[]{:S(2)}) copy-start(f32[32,8,64]{2,1,0:T(8,128)} %copy.91) | copy-start | bytes 196612
  162.2 14.1 %copy-start.19 = (pred[32]{0:T(512)(128)(4,1)S(1)}, pred[32]{0:T(512)(128)(4,1)}, u32[]{:S(2)}) copy-start(pred[32]{0:T(512)(128)(4,1)} %get-tuple-element.83) | copy-start | bytes 100
  170.5 5.8 %copy-start.2 = (f32[32,8,64,64]{3,2,1,0:T(8,128)S(1)}, f32[32,8,64,64]{3,2,1,0:T(8,128)}, u32[]{:S(2)}) copy-start(f32[32,8,64,64]{3,2,1,0:T(8,128)} %reshape.338) | copy-start | bytes 12582916
  170.5 5.8 %copy-start.8 = (f32[32,8,64]{2,1,0:T(8,128)S(1)}, f32[32,8,64]{2,1,0:T(8,128)}, u32[]{:S(2)}) copy-start(f32[32,8,64]{2,1,0:T(8,128)} %get-tuple-element.35) | copy-start | bytes 196612
  170.5 18.2 %copy-start.22 = (pred[32]{0:T(512)(128)(4,1)S(1)}, pred[32]{0:T(512)(128)(4,1)}, u32[]{:S(2)}) copy-start(pred[32]{0:T(512)(128)(4,1)} %get-tuple-element.82) | copy-start | bytes 100
  188.7 19.5 %copy-start.4 = (f32[32,8,64]{2,1,0:T(8,128)S(1)}, f32[32,8,64]{2,1,0:T(8,128)}, u32[]{:S(2)}) copy-start(f32[32,8,64]{2,1,0:T(8,128)} %copy.96) | copy-start | bytes 196612
  188.7 19.5 %copy-start.18 = (pred[32]{0:T(512)(128)(4,1)S(1)}, pred[32]{0:T(512)(128)(4,1)}, u32[]{:S(2)}) copy-start(pred[32]{0:T(512)(128)(4,1)} %get-tuple-element.81) | copy-start | bytes 100
  208.3 13.9 %copy-start.7 = (f32[32,8,64]{2,1,0:T(8,128)S(1)}, f32[32,8,64]{2,1,0:T(8,128)}, u32[]{:S(2)}) copy-start(f32[32,8,64]{2,1,0:T(8,128)} %get-tuple-element.49) | copy-start | bytes 196612
  222.2 19.8 %copy-start.16 = (f32[1,512]{1,0:T(1,128)S(1)}, f32[1,512]{1,0:T(1,128)}, u32[]{:S(2)}) copy-start(f32[1,512]{1,0:T(1,128)} %get-tuple-element.73) | copy-start | bytes 6148
  222.2 19.8 %copy-start.17 = (f32[1,512]{1,0:T(1,128)S(1)}, f32[1,512]{1,0:T(1,128)}, u32[]{:S(2)}) copy-start(f32[1,512]{1,0:T(1,128)} %get-tuple-element.79) | copy-start | bytes 6148
  237.7 7.1 %copy-start.3 = (bf16[32,512]{1,0:T(8,128)(2,1)S(1)}, bf16[32,512]{1,0:T(8,128)(2,1)}, u32[]{:S(2)}) copy-start(bf16[32,512]{1,0:T(8,128)(2,1)} %param.26) | copy-start | bytes 98308
  237.7 13.0 %copy-start.26 = (s32[32]{0:T(128)S(1)}, s32[32]{0:T(128)}, u32[]{:S(2)}) copy-start(s32[32]{0:T(128)} %param.22) | copy-start | bytes 388
  237.7 13.1 %copy-start.24 = (pred[32,4]{0,1:T(4,128)(4,1)S(1)}, pred[32,4]{0,1:T(4,128)(4,1)}, u32[]{:S(2)}) copy-start(pred[32,4]{0,1:T(4,128)(4,1)} %get-tuple-element.84) | copy-start | bytes 388
  246.2 9.4 %all-to-all-start.2 = ((bf16[8,4,512]{2,1,0:T(4,128)(2,1)}), bf16[8,4,512]{2,1,0:T(4,128)(2,1)S(1)}, u32[]{:S(2)}, u32[]{:S(2)}) async-start(bf16[8,4,512]{2,1,0:T(4,128)(2,1)} %reshape.356), calls=%async_computation.3 | async-start | bytes 65536 | tf_op jit(solution)/shard_map/all_to_all | solution.py:156
  250.7 179.8 %reduce-scatter.5.cloned.1.call-start = ((), (), s32[]{:S(2)}) async-start(), calls=%async_computation.7 | async-start | bytes 655360 | tf_op jit(solution)/shard_map/reduce_scatter | solution.py:239
  274.9 8.1 %copy-start.6 = (f32[32,8,64]{2,1,0:T(8,128)S(1)}, f32[32,8,64]{2,1,0:T(8,128)}, u32[]{:S(2)}) copy-start(f32[32,8,64]{2,1,0:T(8,128)} %get-tuple-element.50) | copy-start | bytes 196612
  373.1 9.0 %copy-start.9 = (bf16[32,4,512]{2,1,0:T(4,128)(2,1)S(1)}, bf16[32,4,512]{2,1,0:T(4,128)(2,1)}, u32[]{:S(2)}) copy-start(bf16[32,4,512]{2,1,0:T(4,128)(2,1)} %param.21) | copy-start | bytes 393220
  373.1 25.9 %copy-start.13 = (f32[1,2048]{1,0:T(1,128)S(1)}, f32[1,2048]{1,0:T(1,128)}, u32[]{:S(2)}) copy-start(f32[1,2048]{1,0:T(1,128)} %get-tuple-element.69) | copy-start | bytes 24580
  373.1 25.9 %copy-start.14 = (f32[1,2048]{1,0:T(1,128)S(1)}, f32[1,2048]{1,0:T(1,128)}, u32[]{:S(2)}) copy-start(f32[1,2048]{1,0:T(1,128)} %get-tuple-element.72) | copy-start | bytes 24580
  373.1 26.3 %copy-start.15 = (f32[1,2048]{1,0:T(1,128)S(1)}, f32[1,2048]{1,0:T(1,128)}, u32[]{:S(2)}) copy-start(f32[1,2048]{1,0:T(1,128)} %get-tuple-element.62) | copy-start | bytes 24580
  382.2 24.1 %copy-start.23 = (pred[32]{0:T(512)(128)(4,1)S(1)}, pred[32]{0:T(512)(128)(4,1)}, u32[]{:S(2)}) copy-start(pred[32]{0:T(512)(128)(4,1)} %get-tuple-element.82) | copy-start | bytes 100
  382.2 24.1 %copy-start.25 = (pred[32]{0:T(512)(128)(4,1)S(1)}, pred[32]{0:T(512)(128)(4,1)}, u32[]{:S(2)}) copy-start(pred[32]{0:T(512)(128)(4,1)} %get-tuple-element.80) | copy-start | bytes 100
  406.3 26.0 %copy-start.1 = (bf16[512,2048]{1,0:T(8,128)(2,1)S(1)}, bf16[512,2048]{1,0:T(8,128)(2,1)}, u32[]{:S(2)}) copy-start(bf16[512,2048]{1,0:T(8,128)(2,1)} %param.33) | copy-start | bytes 6291460
Sparse Core Ops, SparseCore 0:
  9.6 36.9 all-gather.1
  244.9 30.9 reduce-scatter.2
  406.4 20.1 reduce-scatter.4
where the time goes:
time: 445 us; the launch traced here: 439 us
  local copies, waits for them, and re-layouts  175 us (39%)
  other arithmetic  112 us (25%)
  blocking collectives  94.6 us (21%)
  matrix products  23 us (5%)
  starting transfers between devices  14.6 us (3%)
  between operations  14.5 us (3%)
  waiting for transfers between devices  5.32 us (1%)
    mul x9, local copies, waits for them, and re-layouts, advance(): wkv_square * decay_now[:, :, None, :]  48.5 us
    mul x10, local copies, waits for them, and re-layouts, advance(): value_now[..., None] * key_now[:, :, None, :]  37.6 us
    mul x4, local copies, waits for them, and re-layouts, advance(): removal[..., None] * (unit_now * alpha_now)[:, :, None, :]  31.6 us
    reduce_sum x2, other arithmetic, advance(): removal = -jnp.sum(wkv_square * unit_now[:, :, None, :], axis=-1)  24.5 us
    reduce_sum x2, other arithmetic, advance(): jnp.sum(updated * recept_now[:, :, None, :], axis=-1)  23.4 us
    dot_general x8, matrix products, project(): return jnp.dot(inputs, weight, preferred_element_type=jnp.float32)  23 us
    select_n x1, other arithmetic, advance(): jnp.where(is_valid[:, None, None, None], updated, wkv_square)  22.3 us
    all_gather x1, blocking collectives, per_device(): lax.all_gather(decay_down, 'mdl', axis=0, tiled=True)  20.2 us
  transfers between devices with their start and end apart: 6, of which 1 were waited for; matrix products, arithmetic and copies ran while one was open for 48% of the time, Pallas kernels for 0%

commit v1 on v0

--- a/solution.py
+++ b/solution.py
@@ -158,7 +158,12 @@
     moved_state = got_state.reshape((sequence_batch_count,) + wkv_state.shape[1:])[placing]
     moved_att = got_att.reshape(sequence_batch_count, local_width)[placing].astype(jnp.bfloat16)
     moved_ffn = got_ffn.reshape(sequence_batch_count, local_width)[placing].astype(jnp.bfloat16)
-    full_tokens = lax.all_gather(tokens, "mdl", axis=2, tiled=True)
+    ring = [tokens]
+    for hop in range(3):
+        ring.append(lax.ppermute(ring[-1], "mdl", [(dev, (dev + 1) % 4) for dev in range(4)]))
+    full_tokens = jnp.roll(
+        jnp.concatenate(ring[::-1], axis=2), (lax.axis_index("mdl") + 1) * ring[0].shape[2], axis=2
+    )
     full_stream = full_tokens.astype(jnp.float32)
     entire_channel_count = full_tokens.shape[2]
     prev_att, prev_ffn = (

time: 445 us -> 438 us (0.984)
  blocking collectives: 94.6 us -> 78.8 us
  waiting for transfers between devices: 5.32 us -> 10.9 us
    all_gather x1 -> x0, blocking collectives: 14.9 us -> none  [per_device(): full_tokens = lax.all_gather(tokens, 'mdl', axis=2, tiled=True)]
    ppermute x0 -> x3, waiting for transfers between devices: none -> 5.54 us  [per_device(): lax.ppermute(ring[-1], 'mdl', [(dev, (dev + 1) % 4) for dev in range(4)])]
  transfers between devices with their start and end apart: 6 -> 9, of which waited for: 1 -> 2; matrix products, arithmetic and copies ran while one was open for 48% -> 49% of each run, Pallas kernels for 0% -> 0%
where the time goes in v1:
time: 438 us; the launch traced here: 431 us
  local copies, waits for them, and re-layouts  178 us (41%)
  other arithmetic  108 us (25%)
  blocking collectives  78.8 us (18%)
  matrix products  23.9 us (5%)
  starting transfers between devices  17.2 us (4%)
  between operations  14.5 us (3%)
  waiting for transfers between devices  10.9 us (2%)
    mul x9, local copies, waits for them, and re-layouts, advance(): wkv_square * decay_now[:, :, None, :]  48.5 us
    mul x10, local copies, waits for them, and re-layouts, advance(): value_now[..., None] * key_now[:, :, None, :]  37.6 us
    mul x4, local copies, waits for them, and re-layouts, advance(): removal[..., None] * (unit_now * alpha_now)[:, :, None, :]  31.6 us
    reduce_sum x2, other arithmetic, advance(): removal = -jnp.sum(wkv_square * unit_now[:, :, None, :], axis=-1)  25.3 us
    dot_general x8, matrix products, project(): return jnp.dot(inputs, weight, preferred_element_type=jnp.float32)  23.9 us
    reduce_sum x2, other arithmetic, advance(): jnp.sum(updated * recept_now[:, :, None, :], axis=-1)  23.7 us
    select_n x1, other arithmetic, advance(): jnp.where(is_valid[:, None, None, None], updated, wkv_square)  22.3 us
    all_gather x1, blocking collectives, per_device(): lax.all_gather(decay_down, 'mdl', axis=0, tiled=True)  19.2 us
  transfers between devices with their start and end apart: 9, of which 2 were waited for; matrix products, arithmetic and copies ran while one was open for 49% of the time, Pallas kernels for 0%

profile of v1, /device:TPU:0, one launch (start us, length us, event | category | flops | bytes accessed | tf_op | source)
XLA Modules:
  0.0 431.0 jit_solution(2686062267503015110)
XLA Ops:
  12.3 5.2 %all-to-all-start.1 = ((bf16[8,4,512]{2,1,0:T(4,128)(2,1)}), bf16[8,4,512]{2,1,0:T(4,128)(2,1)S(1)}, u32[]{:S(2)}, u32[]{:S(2)}) async-start(bf16[8,4,512]{2,1,0:T(4,128)(2,1)} %reshape.354), calls=%async_computation.1 | async-start | bytes 65536 | tf_op jit(solution)/shard_map/all_to_all | solution.py:155
  28.6 19.2 %all_gather.19 = bf16[2048,96]{0,1:T(8,128)(2,1)} all-gather(bf16[512,96]{0,1:T(8,128)(2,1)} %param.34), channel_id=1, replica_groups=mesh['req'=8,'mdl'=4] {'mdl'}, dimensions={0}, use_global_device_ids=true | all-gather | bytes 491520 | tf_op jit(solution)/shard_map/all_gather | solution.py:188
  47.7 16.1 %all_gather.20 = bf16[2048,96]{0,1:T(8,128)(2,1)} all-gather(bf16[512,96]{0,1:T(8,128)(2,1)} %param.36), channel_id=1, replica_groups=mesh['req'=8,'mdl'=4] {'mdl'}, dimensions={0}, use_global_device_ids=true | all-gather | bytes 491520 | tf_op jit(solution)/shard_map/all_gather | solution.py:189
  64.6 3.9 copy.89
  68.6 5.0 %gather_fusion = f32[32,8,4096]{2,1,0:T(8,128)} fusion(f32[32,8,4096]{2,1,0:T(8,128)} %param.24, s32[1024]{0:T(1024)S(1)} %pad_clamp_fusion.1), kind=kCustom, calls=%fused_computation | custom fusion | bytes 8388736 | tf_op jit(solution)/shard_map/gather | solution.py:150
  73.6 4.5 %all-to-all-start = ((f32[8,4,8,4096]{3,2,1,0:T(8,128)}), f32[8,4,8,4096]{3,2,1,0:T(8,128)}, u32[]{:S(2)}, u32[]{:S(2)}) async-start(f32[8,4,8,4096]{3,2,1,0:T(8,128)} %bitcast.175), calls=%async_computation | async-start | bytes 8388608 | tf_op jit(solution)/shard_map/all_to_all | solution.py:154
  78.9 13.6 %all_gather.18 = bf16[32,2048]{1,0:T(8,128)(2,1)S(1)} all-gather(bf16[32,512]{1,0:T(8,128)(2,1)S(1)} %gather_fusion.3), channel_id=1, replica_groups=mesh['req'=8,'mdl'=4] {'mdl'}, dimensions={1}, use_global_device_ids=true | all-gather | bytes 163840 | tf_op jit(solution)/shard_map/all_gather | solution.py:170
  93.8 5.5 %collective-permute-done.2 = bf16[32,4,512]{2,1,0:T(4,128)(2,1)S(1)} collective-permute-done((bf16[32,4,512]{2,1,0:T(4,128)(2,1)S(1)}, bf16[32,4,512]{2,1,0:T(4,128)(2,1)S(1)}, u32[]{:S(2)}, u32[]{:S(2)}) %collective-permute-start.2) | collective-permute-done | bytes 131104 | tf_op jit(solution)/shard_map/ppermute | solution.py:163
  102.1 3.9 add_convert_fusion.5
  107.2 2.0 fusion.61
  110.3 2.0 reshape.340
  115.1 1.9 reshape.348
  117.0 1.9 reshape.342
  119.0 2.4 broadcast_add_fusion
  121.5 3.2 fusion.39
  129.2 3.8 broadcast_multiply_fusion.8
  147.0 2.3 fusion.23
  149.3 5.1 %gather_fusion.1 = f32[32,8,4096]{2,1,0:T(8,128)} fusion(f32[32,8,4096]{2,1,0:T(8,128)} %bitcast.1, s32[1024]{0:T(1024)} %copy-done.17), kind=kCustom, calls=%fused_computation.1 | custom fusion | bytes 8388736 | tf_op jit(solution)/shard_map/gather | solution.py:158
  154.5 7.9 %reshape.338 = f32[32,8,64,64]{3,2,1,0:T(8,128)} reshape(f32[32,8,4096]{2,1,0:T(8,128)} %gather_fusion.1) | data formatting | bytes 8388608 | tf_op jit(solution)/shard_map/reshape | solution.py:61
  162.3 5.8 %multiply_reduce_fusion.7 = f32[32,8,64]{2,1,0:T(8,128)S(1)} fusion(f32[32,8,64,64]{3,2,1,0:T(8,128)} %reshape.338, f32[32,8,64]{2,1,0:T(8,128)S(1)} %get-tuple-element.90), kind=kLoop, calls=%fused_computation.16 | loop fusion | flops 2080768 | bytes 4325376 | tf_op jit(solution)/shard_map/reduce_sum | solution.py:25
  168.2 11.0 %multiply_reduce_fusion.6 = (f32[32,8,64]{2,1,0:T(8,128)S(1)}, f32[32,8,64]{2,1,0:T(8,128)S(1)}) fusion(f32[32,8,64]{2,1,0:T(8,128)S(1)} %copy-done.11, f32[32,8,64,64]{3,2,1,0:T(8,128)S(1)} %copy-done.2, f32[32,8,64]{2,1,0:T(8,128)S(1)} %get-tuple-element.51, f32[32,8,64]{2,1,0:T(8,128)S(1)} %get-tuple-element.30, f32[32,8,64]{2,1,0:T(8,128)S(1)} %neg.38, ...), kind=kLoop, calls=%fused_computation.14 | loop fusion | flops 10452992 | bytes 4784160 | tf_op jit(solution)/shard_map/reduce_sum | solution.py:31
  180.5 19.5 %multiply_reduce_fusion.3 = (f32[32,8,64]{2,1,0:T(8,128)S(1)}, f32[32,8,64,64]{3,2,1,0:T(8,128)}, f32[32,8,64]{2,1,0:T(8,128)S(1)}, f32[32,8,64,64]{3,2,1,0:T(8,...) fusion(f32[32,8,64]{2,1,0:T(8,128)} %get-tuple-element.92, ...), kind=kLoop, calls=%fused_computation.10 | loop fusion | flops 16744448 | bytes 26083392 | tf_op jit(solution)/shard_map/reduce_sum | solution.py:25
  200.8 12.8 %multiply_reduce_fusion.2 = (f32[32,8,64]{2,1,0:T(8,128)S(1)}, f32[32,8,64]{2,1,0:T(8,128)S(1)}, f32[32,8,64,64]{3,2,1,0:T(8,128)}, f32[32,8,64,64]{3,2,1,0:T(8,128)}) fusion(f32[32,8,64]{2,1,0:T(8,128)} %get-tuple-element.34, f32[32,8,64,64]{3,2,1,0:T(8,128)} %get-tuple-element.18, f32[32,8,64]{2,1,0:T(8,128)S(1)} %get-tuple-element.48, ...), kind=kLoop, calls=%fused_computation.8 | loop fusion | flops 10452992 | bytes 13172768 | tf_op jit(solution)/shard_map/reduce_sum | solution.py:31
  215.0 15.7 %broadcast_multiply_fusion.1 = (f32[32,8,64,64]{3,2,1,0:T(8,128)}, f32[32,8,64]{2,1,0:T(8,128)S(1)}, f32[32,8,64,64]{3,2,1,0:T(8,128)}) fusion(f32[32,8,64]{2,1,0:T(8,128)} %get-tuple-element.31, f32[32,8,64]{2,1,0:T(8,128)} %neg.42, f32[32,8,64]{2,1,0:T(8,128)} %get-tuple-element.33, f32[32,8,64]{2,1,0:T(8,128)} %get-tuple-element.40, ...), kind=kLoop, calls=%fused_computation.19 | loop fusion | flops 13615104 | bytes 13369376 | tf_op jit(solution)/shard_map/mul | solution.py:28
  235.0 2.8 fusion.19
  239.2 4.1 all-to-all-start.2
  243.5 4.6 %all-to-all-done.2 = bf16[8,4,512]{2,1,0:T(4,128)(2,1)S(1)} async-done(((bf16[8,4,512]{2,1,0:T(4,128)(2,1)}), bf16[8,4,512]{2,1,0:T(4,128)(2,1)S(1)}, u32[]{:S(2)}, u32[]{:S(2)}) %all-to-all-start.2) | async-done | bytes 32800 | tf_op jit(solution)/shard_map/all_to_all | solution.py:156
  248.9 14.9 %all_gather.23 = bf16[32,2048]{1,0:T(8,128)(2,1)S(1)} all-gather(bf16[32,512]{1,0:T(8,128)(2,1)S(1)} %gather_fusion.5), channel_id=1, replica_groups=mesh['req'=8,'mdl'=4] {'mdl'}, dimensions={1}, use_global_device_ids=true | all-gather | bytes 163840 | tf_op jit(solution)/shard_map/all_gather | solution.py:171
  264.1 3.7 mul.601
  267.8 8.1 %mul.651 = f32[32,8,4096]{2,1,0:T(8,128)} reshape(f32[32,8,64,64]{3,2,1,0:T(8,128)} %mul.601) | data formatting | bytes 8388608 | tf_op jit(solution)/shard_map/mul | solution.py:27
  275.9 3.7 mul.565
  279.6 7.9 %mul.643 = f32[32,8,4096]{2,1,0:T(8,128)} reshape(f32[32,8,64,64]{3,2,1,0:T(8,128)} %mul.565) | data formatting | bytes 8388608 | tf_op jit(solution)/shard_map/mul | solution.py:27
  287.5 3.7 mul.583
  291.2 7.9 %mul.647 = f32[32,8,4096]{2,1,0:T(8,128)} reshape(f32[32,8,64,64]{3,2,1,0:T(8,128)} %mul.583) | data formatting | bytes 8388608 | tf_op jit(solution)/shard_map/mul | solution.py:27
  299.1 3.7 mul.527
  302.9 7.9 %mul.639 = f32[32,8,4096]{2,1,0:T(8,128)} reshape(f32[32,8,64,64]{3,2,1,0:T(8,128)} %mul.527) | data formatting | bytes 8388608 | tf_op jit(solution)/shard_map/mul | solution.py:27
  310.7 7.9 %mul.641 = f32[32,8,4096]{2,1,0:T(8,128)} reshape(f32[32,8,64,64]{3,2,1,0:T(8,128)} %get-tuple-element.52) | data formatting | bytes 8388608 | tf_op jit(solution)/shard_map/mul | solution.py:28
  318.6 7.9 %mul.642 = f32[32,8,4096]{2,1,0:T(8,128)} reshape(f32[32,8,64,64]{3,2,1,0:T(8,128)} %get-tuple-element.53) | data formatting | bytes 8388608 | tf_op jit(solution)/shard_map/mul | solution.py:29
  326.5 7.9 %mul.645 = f32[32,8,4096]{2,1,0:T(8,128)} reshape(f32[32,8,64,64]{3,2,1,0:T(8,128)} %get-tuple-element.54) | data formatting | bytes 8388608 | tf_op jit(solution)/shard_map/mul | solution.py:28
  334.4 7.9 %mul.646 = f32[32,8,4096]{2,1,0:T(8,128)} reshape(f32[32,8,64,64]{3,2,1,0:T(8,128)} %get-tuple-element.55) | data formatting | bytes 8388608 | tf_op jit(solution)/shard_map/mul | solution.py:29
  342.3 7.9 %mul.649 = f32[32,8,4096]{2,1,0:T(8,128)} reshape(f32[32,8,64,64]{3,2,1,0:T(8,128)} %get-tuple-element.56) | data formatting | bytes 8388608 | tf_op jit(solution)/shard_map/mul | solution.py:28
  350.2 7.9 %mul.650 = f32[32,8,4096]{2,1,0:T(8,128)} reshape(f32[32,8,64,64]{3,2,1,0:T(8,128)} %get-tuple-element.57) | data formatting | bytes 8388608 | tf_op jit(solution)/shard_map/mul | solution.py:29
  358.1 7.9 %mul.653 = f32[32,8,4096]{2,1,0:T(8,128)} reshape(f32[32,8,64,64]{3,2,1,0:T(8,128)} %get-tuple-element.58) | data formatting | bytes 8388608 | tf_op jit(solution)/shard_map/mul | solution.py:28
  366.0 7.9 %mul.654 = f32[32,8,4096]{2,1,0:T(8,128)} reshape(f32[32,8,64,64]{3,2,1,0:T(8,128)} %get-tuple-element.60) | data formatting | bytes 8388608 | tf_op jit(solution)/shard_map/mul | solution.py:29
  375.1 15.0 %all_gather.22 = bf16[32,4,2048]{2,1,0:T(4,128)(2,1)S(1)} all-gather(bf16[32,4,512]{2,1,0:T(4,128)(2,1)S(1)} %add_convert_fusion.6), channel_id=1, replica_groups=mesh['req'=8,'mdl'=4] {'mdl'}, dimensions={2}, use_global_device_ids=true | all-gather | bytes 655360 | tf_op jit(solution)/shard_map/all_gather | solution.py:232
  392.6 5.6 %convolution_convert_fusion = bf16[128,2048]{1,0:T(8,128)(2,1)} fusion(bf16[1024,2048]{1,0:T(8,128)(2,1)} %param.41, bf16[128,2048]{1,0:T(8,128)(2,1)S(1)} %reshape.351, bf16[2048,1024]{1,0:T(8,128)(2,1)} %param.40), kind=kOutput, calls=%fused_computation.29 | convolution fusion | flops 1074397184 | bytes 9437184 | tf_op jit(solution)/shard_map/dot_general | solution.py:14
  398.2 22.3 %add_select_fusion = f32[32,8,4096]{2,1,0:T(8,128)} fusion(f32[32,8,4096]{2,1,0:T(8,128)} %mul.654, f32[32,8,4096]{2,1,0:T(8,128)} %mul.653, f32[32,8,4096]{2,1,0:T(8,128)} %mul.651, f32[32,8,4096]{2,1,0:T(8,128)} %mul.650, f32[32,8,4096]{2,1,0:T(8,128)} %mul.649, f32[32,8,4096]{2,1,0:T(8,128)} %mul.647, f32[32,8,4096]{2,1,0:T(8,128)} %mul.646, ...), kind=kLoop, calls=%fused_computation.17 | loop fusion | flops 16777216 | bytes 58720384 | tf_op jit(solution)/shard_map/jit(_where)/select_n | solution.py:32
  420.5 2.0 multiply_reduce_fusion.10
  (166 shorter events, 61.1 us)
Async XLA Ops:
  7.2 227.8 %copy-start = (bf16[512,2048]{1,0:T(8,128)(2,1)S(1)}, bf16[512,2048]{1,0:T(8,128)(2,1)}, u32[]{:S(2)}) copy-start(bf16[512,2048]{1,0:T(8,128)(2,1)} %param.33) | copy-start | bytes 6291460
  7.2 139.8 %all-gather.2.cloned.1.call-start = ((), (), s32[]{:S(2)}) async-start(), calls=%async_computation.5 | async-start | bytes 1310720 | tf_op jit(solution)/shard_map/all_gather | solution.py:190
  10.3 63.3 %copy-start.16 = (s32[1024]{0:T(1024)}, s32[1024]{0:T(1024)S(1)}, u32[]{:S(2)}) copy-start(s32[1024]{0:T(1024)S(1)} %pad_clamp_fusion.1) | copy-start | bytes 12292
  12.3 61.3 %all-to-all-start.1 = ((bf16[8,4,512]{2,1,0:T(4,128)(2,1)}), bf16[8,4,512]{2,1,0:T(4,128)(2,1)S(1)}, u32[]{:S(2)}, u32[]{:S(2)}) async-start(bf16[8,4,512]{2,1,0:T(4,128)(2,1)} %reshape.354), calls=%async_computation.1 | async-start | bytes 65536 | tf_op jit(solution)/shard_map/all_to_all | solution.py:155
  17.5 46.3 %collective-permute-start = (bf16[32,4,512]{2,1,0:T(4,128)(2,1)}, bf16[32,4,512]{2,1,0:T(4,128)(2,1)S(1)}, u32[]{:S(2)}, u32[]{:S(2)}) collective-permute-start(bf16[32,4,512]{2,1,0:T(4,128)(2,1)} %param.21), channel_id=1, source_target_pairs={{0,1},{1,2},{2,3},{3,0},{4,5},{5,6},{6,7},{7,4},{8,9},{9,10},{10,1... | collective-permute-start | bytes 393224 | tf_op jit(solution)/shard_map/ppermute | solution.py:163
  63.8 28.7 %collective-permute-start.1 = (bf16[32,4,512]{2,1,0:T(4,128)(2,1)S(1)}, bf16[32,4,512]{2,1,0:T(4,128)(2,1)S(1)}, u32[]{:S(2)}, u32[]{:S(2)}) collective-permute-start(bf16[32,4,512]{2,1,0:T(4,128)(2,1)S(1)} %collective-permute-done), channel_id=1, source_target_pairs={{0,1},{1,2},{2,3},{3,0},{4,5},{5,6},{6,7},{7,4},{8,9},{9,10},{10,1... | collective-permute-start | bytes 393224 | tf_op jit(solution)/shard_map/ppermute | solution.py:163
  64.6 13.6 %copy-start.17 = (s32[1024]{0:T(1024)}, s32[1024]{0:T(1024)S(1)}, u32[]{:S(2)}) copy-start(s32[1024]{0:T(1024)S(1)} %pad_clamp_fusion) | copy-start | bytes 12292
  68.6 30.9 %copy-start.9 = (bf16[32,4,512]{2,1,0:T(4,128)(2,1)S(1)}, bf16[32,4,512]{2,1,0:T(4,128)(2,1)}, u32[]{:S(2)}) copy-start(bf16[32,4,512]{2,1,0:T(4,128)(2,1)} %param.21) | copy-start | bytes 393220
  73.6 75.7 %all-to-all-start = ((f32[8,4,8,4096]{3,2,1,0:T(8,128)}), f32[8,4,8,4096]{3,2,1,0:T(8,128)}, u32[]{:S(2)}, u32[]{:S(2)}) async-start(f32[8,4,8,4096]{3,2,1,0:T(8,128)} %bitcast.175), calls=%async_computation | async-start | bytes 8388608 | tf_op jit(solution)/shard_map/all_to_all | solution.py:154
  78.2 295.8 %reduce-scatter.3.cloned.1.call-start = ((), (), s32[]{:S(2)}) async-start(), calls=%async_computation.6 | async-start | bytes 1310720 | tf_op jit(solution)/shard_map/reduce_scatter | solution.py:228
  92.5 6.8 %collective-permute-start.2 = (bf16[32,4,512]{2,1,0:T(4,128)(2,1)S(1)}, bf16[32,4,512]{2,1,0:T(4,128)(2,1)S(1)}, u32[]{:S(2)}, u32[]{:S(2)}) collective-permute-start(bf16[32,4,512]{2,1,0:T(4,128)(2,1)S(1)} %collective-permute-done.1), channel_id=1, source_target_pairs={{0,1},{1,2},{2,3},{3,0},{4,5},{5,6},{6,7},{7,4},{8,9},{9,10},{10,1... | collective-permute-start | bytes 393224 | tf_op jit(solution)/shard_map/ppermute | solution.py:163
  93.5 18.8 %copy-start.22 = (bf16[96,512]{1,0:T(8,128)(2,1)S(1)}, bf16[96,512]{1,0:T(8,128)(2,1)}, u32[]{:S(2)}) copy-start(bf16[96,512]{1,0:T(8,128)(2,1)} %param.35) | copy-start | bytes 294916
  101.1 1.0 copy-start.3
  154.5 13.7 %copy-start.6 = (f32[32,8,64]{2,1,0:T(8,128)S(1)}, f32[32,8,64]{2,1,0:T(8,128)}, u32[]{:S(2)}) copy-start(f32[32,8,64]{2,1,0:T(8,128)} %copy.91) | copy-start | bytes 196612
  162.3 5.8 %copy-start.2 = (f32[32,8,64,64]{3,2,1,0:T(8,128)S(1)}, f32[32,8,64,64]{3,2,1,0:T(8,128)}, u32[]{:S(2)}) copy-start(f32[32,8,64,64]{3,2,1,0:T(8,128)} %reshape.338) | copy-start | bytes 12582916
  162.3 5.8 %copy-start.11 = (f32[32,8,64]{2,1,0:T(8,128)S(1)}, f32[32,8,64]{2,1,0:T(8,128)}, u32[]{:S(2)}) copy-start(f32[32,8,64]{2,1,0:T(8,128)} %get-tuple-element.35) | copy-start | bytes 196612
  162.3 5.8 %copy-start.14 = (pred[32]{0:T(512)(128)(4,1)S(1)}, pred[32]{0:T(512)(128)(4,1)}, u32[]{:S(2)}) copy-start(pred[32]{0:T(512)(128)(4,1)} %get-tuple-element.83) | copy-start | bytes 100
  180.5 20.3 %copy-start.5 = (f32[32,8,64]{2,1,0:T(8,128)S(1)}, f32[32,8,64]{2,1,0:T(8,128)}, u32[]{:S(2)}) copy-start(f32[32,8,64]{2,1,0:T(8,128)} %copy.96) | copy-start | bytes 196612
  200.8 14.2 %copy-start.8 = (f32[32,8,64]{2,1,0:T(8,128)S(1)}, f32[32,8,64]{2,1,0:T(8,128)}, u32[]{:S(2)}) copy-start(f32[32,8,64]{2,1,0:T(8,128)} %get-tuple-element.49) | copy-start | bytes 196612
  230.7 7.1 %copy-start.4 = (bf16[32,512]{1,0:T(8,128)(2,1)S(1)}, bf16[32,512]{1,0:T(8,128)(2,1)}, u32[]{:S(2)}) copy-start(bf16[32,512]{1,0:T(8,128)(2,1)} %param.26) | copy-start | bytes 98308
  230.7 12.6 %copy-start.21 = (s32[32]{0:T(128)S(1)}, s32[32]{0:T(128)}, u32[]{:S(2)}) copy-start(s32[32]{0:T(128)} %param.22) | copy-start | bytes 388
  230.7 12.7 %copy-start.19 = (pred[32,4]{0,1:T(4,128)(4,1)S(1)}, pred[32,4]{0,1:T(4,128)(4,1)}, u32[]{:S(2)}) copy-start(pred[32,4]{0,1:T(4,128)(4,1)} %get-tuple-element.84) | copy-start | bytes 388
  239.2 8.9 %all-to-all-start.2 = ((bf16[8,4,512]{2,1,0:T(4,128)(2,1)}), bf16[8,4,512]{2,1,0:T(4,128)(2,1)S(1)}, u32[]{:S(2)}, u32[]{:S(2)}) async-start(bf16[8,4,512]{2,1,0:T(4,128)(2,1)} %reshape.356), calls=%async_computation.3 | async-start | bytes 65536 | tf_op jit(solution)/shard_map/all_to_all | solution.py:156
  243.2 179.2 %reduce-scatter.5.cloned.1.call-start = ((), (), s32[]{:S(2)}) async-start(), calls=%async_computation.7 | async-start | bytes 655360 | tf_op jit(solution)/shard_map/reduce_scatter | solution.py:244
  267.8 8.1 %copy-start.7 = (f32[32,8,64]{2,1,0:T(8,128)S(1)}, f32[32,8,64]{2,1,0:T(8,128)}, u32[]{:S(2)}) copy-start(f32[32,8,64]{2,1,0:T(8,128)} %get-tuple-element.50) | copy-start | bytes 196612
  366.0 9.0 %copy-start.10 = (bf16[32,4,512]{2,1,0:T(4,128)(2,1)S(1)}, bf16[32,4,512]{2,1,0:T(4,128)(2,1)}, u32[]{:S(2)}) copy-start(bf16[32,4,512]{2,1,0:T(4,128)(2,1)} %param.21) | copy-start | bytes 393220
  366.0 25.3 %copy-start.12 = (f32[1,2048]{1,0:T(1,128)S(1)}, f32[1,2048]{1,0:T(1,128)}, u32[]{:S(2)}) copy-start(f32[1,2048]{1,0:T(1,128)} %get-tuple-element.62) | copy-start | bytes 24580
  375.1 23.1 %copy-start.13 = (pred[32]{0:T(512)(128)(4,1)S(1)}, pred[32]{0:T(512)(128)(4,1)}, u32[]{:S(2)}) copy-start(pred[32]{0:T(512)(128)(4,1)} %get-tuple-element.81) | copy-start | bytes 100
  375.1 23.1 %copy-start.15 = (pred[32]{0:T(512)(128)(4,1)S(1)}, pred[32]{0:T(512)(128)(4,1)}, u32[]{:S(2)}) copy-start(pred[32]{0:T(512)(128)(4,1)} %get-tuple-element.83) | copy-start | bytes 100
  375.1 23.1 %copy-start.18 = (pred[32]{0:T(512)(128)(4,1)S(1)}, pred[32]{0:T(512)(128)(4,1)}, u32[]{:S(2)}) copy-start(pred[32]{0:T(512)(128)(4,1)} %get-tuple-element.82) | copy-start | bytes 100
  375.1 23.1 %copy-start.20 = (pred[32]{0:T(512)(128)(4,1)S(1)}, pred[32]{0:T(512)(128)(4,1)}, u32[]{:S(2)}) copy-start(pred[32]{0:T(512)(128)(4,1)} %get-tuple-element.80) | copy-start | bytes 100
  398.2 26.0 %copy-start.1 = (bf16[512,2048]{1,0:T(8,128)(2,1)S(1)}, bf16[512,2048]{1,0:T(8,128)(2,1)}, u32[]{:S(2)}) copy-start(bf16[512,2048]{1,0:T(8,128)(2,1)} %param.33) | copy-start | bytes 6291460
Sparse Core Ops, SparseCore 0:
  9.6 39.4 all-gather.1
  237.9 28.3 reduce-scatter.2
  398.3 19.6 reduce-scatter.4
